TPU v7x, 32 devices: a whole 2x2x4 slice. The times are simulated.
32 devices in a mesh: group: 4 (over x, core), mp: 8 (over z, y).
Axes of the slice: x: 2, y: 2, z: 4, core: 2. Of those that a mesh axis runs over, the one named last changes fastest.
Arguments:
- tokens: bfloat16 [4096, 8192], P(('group', 'mp')), may hold values from -36 to 36
- cached_update: bfloat16 [4096, 8192], P('group', 'mp'), may hold values from -3 to 3
- norm_gain: float32 [8192], replicated, may hold values from 0.25 to 1.75
- gate_weight: bfloat16 [8192, 14336], P('group', 'mp'), may hold values from -0.0625 to 0.0625
- up_weight: bfloat16 [8192, 14336], P('group', 'mp'), may hold values from -0.0625 to 0.0625
- down_weight: bfloat16 [14336, 8192], P('mp', 'group'), may hold values from -0.0625 to 0.0625
- stale_blocks: int32 [4, 2], P('group'), may hold values from -1 to 7, as said below
- stale_count: int32 [4], replicated, may hold values from 0 to 2, as said below
- lengths: int32 [4], P('group'), may hold values from 512 to 1024, as said below
Outputs:
- refreshed: bfloat16 [4096, 8192], P('group', 'mp')
Inputs may be any that keep to these rules, and one draw needn't show every extreme that they name: `stale_count`: the counts sum to exactly 4. At least a quarter of the groups have 2, at least a quarter have none. A group's count never exceeds the number of its blocks that begin below its length. `stale_blocks`: row g holds stale_count[g] distinct block numbers, each of a block that begins below lengths[g], in any order, then -1 in the other places. Some group lists block 7. `lengths`: some request has 1024 tokens.
All inputs are finite; a program needn't handle non-finite values.
Results may differ from a plain program's by a relative error of at most 0.0035.
Values may be sent and summed in bfloat16 or wider, within the bound.
A program may use at most 256 MiB of HBM per device.

v0:
```python
import jax
import jax.numpy as jnp
from jax import lax
from jax.sharding import PartitionSpec as P

BLK = 128


epsilon = 1e-05


def normalize(row_data, norm_gain):
    values = row_data.astype(jnp.float32)
    mean_sq = jnp.mean(values * values, axis=-1, keepdims=True)
    return (values * lax.rsqrt(mean_sq + epsilon) * norm_gain).astype(jnp.bfloat16)


def refresh(slots, norm_gain, gate_weight, up_weight, down_weight):
    slot_count = slots.shape[0]
    full_rows = lax.all_gather(slots, "mp", axis=2, tiled=True)
    row_data = full_rows.reshape(slot_count * BLK, full_rows.shape[2])
    normed = normalize(row_data, norm_gain)
    gate_vals = jnp.dot(
        normed,
        lax.all_gather(gate_weight, "group", axis=0, tiled=True),
        preferred_element_type=jnp.float32,
    )
    up_vals = jnp.dot(
        normed,
        lax.all_gather(up_weight, "group", axis=0, tiled=True),
        preferred_element_type=jnp.float32,
    )
    hidden = (jax.nn.silu(gate_vals) * up_vals).astype(jnp.bfloat16)
    partial_value = jnp.dot(
        hidden,
        lax.all_gather(down_weight, "group", axis=1, tiled=True),
        preferred_element_type=jnp.float32,
    )
    update = lax.psum_scatter(
        partial_value.astype(jnp.bfloat16), "mp", scatter_dimension=1, tiled=True
    ).astype(jnp.float32)
    return update.reshape(slot_count, BLK, update.shape[1])


def body(
    tokens,
    cached_update,
    norm_gain,
    gate_weight,
    up_weight,
    down_weight,
    stale_blocks,
    stale_count,
    lengths,
):
    n_group = lax.axis_size("group")
    columns = lax.all_to_all(tokens, "mp", split_axis=1, concat_axis=0, tiled=True)
    seq_rows, col_width = columns.shape
    block_total = seq_rows // BLK
    column_blocks = columns.reshape(block_total, BLK, col_width)
    group_id = lax.axis_index("group")
    group_ids = jnp.arange(n_group, dtype=jnp.int32)
    own_mask = group_ids == group_id
    own_count = jnp.sum(jnp.where(own_mask, stale_count, 0))
    own_list = stale_blocks[0]
    list_size = stale_blocks.shape[1]
    block_ids = jnp.arange(block_total, dtype=jnp.int32)
    picker = (own_list[:, None] == block_ids[None, :]).astype(jnp.bfloat16)
    own_rows = jnp.einsum(
        "pb,brc->prc", picker, column_blocks, preferred_element_type=jnp.float32
    ).astype(jnp.bfloat16)
    results = refresh(own_rows, norm_gain, gate_weight, up_weight, down_weight)
    positions = jnp.arange(list_size, dtype=jnp.int32)
    listed = (own_list[None, :] == block_ids[:, None]) & (positions[None, :] < own_count)
    block_update = jnp.einsum(
        "bp,prc->brc", listed.astype(jnp.float32), results, precision=lax.Precision.HIGHEST
    )
    stale_rows = jnp.any(listed, axis=1)[:, None, None]
    row_pos = block_ids[:, None] * BLK + jnp.arange(BLK, dtype=jnp.int32)[None, :]
    live_rows = (row_pos < lengths[0])[:, :, None]
    cache_blocks = cached_update.reshape(block_total, BLK, col_width).astype(jnp.float32)
    combined = column_blocks.astype(jnp.float32) + jnp.where(stale_rows, block_update, cache_blocks)
    refreshed = jnp.where(live_rows, combined, jnp.float32(0.0))
    return refreshed.astype(jnp.bfloat16).reshape(seq_rows, col_width)


def solution(mesh):
    in_specs = (
        P(("group", "mp"), None),
        P("group", "mp"),
        P(),
        P("group", "mp"),
        P("group", "mp"),
        P("mp", "group"),
        P("group", None),
        P(),
        P("group"),
    )
    out_specs = P("group", "mp")
    return jax.shard_map(body, mesh=mesh, in_specs=in_specs, out_specs=out_specs, check_vma=False)
```

profile of v0, /device:TPU:2, one launch (start us, length us, event | category | flops | bytes accessed | tf_op | source)
XLA Modules:
  0.0 815.4 jit_solution(3097391666787981656)
XLA Ops:
  6.5 0.0 all-gather.5.cloned.1.call-start
  6.5 4.1 copy.28
  10.6 0.0 copy-start.4
  10.6 2.9 copy.29
  13.5 53.9 %all_to_all.16 = bf16[128,8,1024]{2,0,1:T(8,128)(2,1)S(1)} all-to-all(bf16[128,8,1024]{2,0,1:T(8,128)(2,1)S(1)} %copy.29), channel_id=1, replica_groups=mesh['group'=4,'mp'=8] {'mp'}, dimensions={1} | all-to-all | bytes 4194304 | tf_op jit(solution)/shard_map/all_to_all | solution.py:57
  67.3 0.0 copy-start.1
  67.3 1.3 copy-done.1
  68.7 0.0 copy-done.4
  68.7 1.4 fusion.6
  70.1 0.9 copy.53
  71.1 0.0 all-gather.5.cloned.1.call-update
  71.1 0.0 all-gather.7.cloned.1.call-start
  71.1 0.7 all-gather.7.cloned.1.call-update
  71.8 0.0 all-gather.11.cloned.1.call-start
  71.9 0.7 all-gather.11.cloned.1.call-update
  72.6 0.0 copy-start.3
  72.6 0.0 all-gather.9.cloned.1.call-start
  72.6 0.5 all-gather.9.cloned.1.call-update
  73.2 0.2 reduce-scatter.2.cloned.1.call-start
  73.4 69.6 %all-gather.5.cloned.1.call-done = bf16[2,128,8192]{2,1,0:T(8,128)(2,1)} async-done(((bf16[2,128,1024]{2,1,0:T(8,128)(2,1)}), bf16[2,128,8192]{2,1,0:T(8,128)(2,1)}) %all-gather.5.cloned.1.call-update) | async-done | bytes 4194320 | tf_op jit(solution)/shard_map/all_gather | solution.py:20
  143.0 0.0 copy-start
  143.0 3.3 multiply_reduce_fusion
  146.3 0.0 copy-done.3
  146.3 0.2 copy-done
  146.4 3.1 fusion.1
  149.6 170.4 %all-gather.7.cloned.1.call-done = bf16[8192,1792]{1,0:T(8,128)(2,1)} async-done(((bf16[2048,1792]{1,0:T(8,128)(2,1)}), bf16[8192,1792]{1,0:T(8,128)(2,1)}) %all-gather.7.cloned.1.call-update) | async-done | bytes 29360144 | tf_op jit(solution)/shard_map/all_gather | solution.py:25
  320.0 16.3 %fusion.26 = f32[256,1792]{1,0:T(8,128)S(1)} fusion(bf16[256,8192]{1,0:T(8,128)(2,1)} %fusion.1, bf16[8192,1792]{1,0:T(8,128)(2,1)} %all-gather.7.cloned.1.call-done), kind=kOutput, calls=%fused_computation.38 | convolution fusion | flops 7516192768 | bytes 35389440 | tf_op jit(solution)/shard_map/dot_general | solution.py:23
  336.2 163.3 %all-gather.11.cloned.1.call-done = bf16[1792,8192]{1,0:T(8,128)(2,1)} async-done(((bf16[1792,2048]{1,0:T(8,128)(2,1)}), bf16[1792,8192]{1,0:T(8,128)(2,1)}) %all-gather.11.cloned.1.call-update) | async-done | bytes 29360144 | tf_op jit(solution)/shard_map/all_gather | solution.py:36
  499.6 179.4 %all-gather.9.cloned.1.call-done = bf16[8192,1792]{1,0:T(8,128)(2,1)} async-done(((bf16[2048,1792]{1,0:T(8,128)(2,1)}), bf16[8192,1792]{1,0:T(8,128)(2,1)}) %all-gather.9.cloned.1.call-update) | async-done | bytes 29360144 | tf_op jit(solution)/shard_map/all_gather | solution.py:30
  679.0 29.4 %convolution_convert_fusion = bf16[256,8192]{1,0:T(8,128)(2,1)} fusion(bf16[1792,8192]{1,0:T(8,128)(2,1)} %all-gather.11.cloned.1.call-done, bf16[256,8192]{1,0:T(8,128)(2,1)} %fusion.1, bf16[8192,1792]{1,0:T(8,128)(2,1)} %all-gather.9.cloned.1.call-done, f32[256,1792]{1,0:T(8,128)S(1)} %fusion.26), kind=kOutput, calls=%fused_computation | convolution fusion | flops 15037235200 | bytes 68943872 | tf_op jit(solution)/shard_map/dot_general | solution.py:34
  708.4 0.0 reduce-scatter.2.cloned.1.call-update
  708.4 0.0 copy-start.6
  708.4 0.0 copy-start.5
  708.4 0.0 copy-start.2
  708.5 4.2 convert.2
  713.3 0.0 copy-done.6
  713.3 0.6 fusion.22
  713.9 0.5 iota_compare_fusion
  714.4 0.0 copy-done.5
  714.5 0.1 fusion.20
  714.6 83.8 %reduce-scatter.2.cloned.1.call-done = bf16[256,1024]{1,0:T(8,128)(2,1)} async-done(((bf16[256,8192]{1,0:T(8,128)(2,1)}), bf16[256,1024]{1,0:T(8,128)(2,1)}) %reduce-scatter.2.cloned.1.call-update) | async-done | bytes 524304 | tf_op jit(solution)/shard_map/reduce_scatter | solution.py:39
  798.4 0.0 copy-done.2
  798.4 8.0 fusion.4
  806.4 2.5 copy.36
  (3 shorter events, 0.0 us)
Async XLA Ops:
  6.5 136.5 %all-gather.5.cloned.1.call-start = ((), (), s32[]{:S(2)}) async-start(), calls=%async_computation.2 | async-start | bytes 4718592 | tf_op jit(solution)/shard_map/all_gather | solution.py:20
  10.6 58.1 %copy-start.4 = (s32[1,2]{1,0:T(1,128)S(1)}, s32[1,2]{1,0:T(1,128)}, u32[]{:S(2)}) copy-start(s32[1,2]{1,0:T(1,128)} %param.15) | copy-start | bytes 28
  67.3 1.3 copy-start.1
  71.1 248.9 %all-gather.7.cloned.1.call-start = ((), (), s32[]{:S(2)}) async-start(), calls=%async_computation.3 | async-start | bytes 36700160 | tf_op jit(solution)/shard_map/all_gather | solution.py:25
  71.8 427.8 %all-gather.11.cloned.1.call-start = ((), (), s32[]{:S(2)}) async-start(), calls=%async_computation.5 | async-start | bytes 36700160 | tf_op jit(solution)/shard_map/all_gather | solution.py:36
  72.6 73.7 %copy-start.3 = (f32[8192]{0:T(1024)S(1)}, f32[8192]{0:T(1024)}, u32[]{:S(2)}) copy-start(f32[8192]{0:T(1024)} %param.11) | copy-start | bytes 98308
  72.6 606.5 %all-gather.9.cloned.1.call-start = ((), (), s32[]{:S(2)}) async-start(), calls=%async_computation.4 | async-start | bytes 36700160 | tf_op jit(solution)/shard_map/all_gather | solution.py:30
  73.2 725.2 %reduce-scatter.2.cloned.1.call-start = ((), (), s32[]{:S(2)}) async-start(), calls=%async_computation.6 | async-start | bytes 4718592 | tf_op jit(solution)/shard_map/reduce_scatter | solution.py:39
  143.0 3.4 copy-start
  708.4 4.9 copy-start.6
  708.4 6.0 copy-start.5
  708.4 90.0 %copy-start.2 = (bf16[128,8,1024]{2,0,1:T(8,128)(2,1)S(1)}, bf16[128,8,1024]{2,0,1:T(8,128)(2,1)}, u32[]{:S(2)}) copy-start(bf16[128,8,1024]{2,0,1:T(8,128)(2,1)} %copy-done.1) | copy-start | bytes 6291460
Sparse Core Ops, SparseCore 0:
  71.2 71.7 all-gather.4
  144.6 175.3 all-gather.6
  321.6 177.9 all-gather.10
  501.0 177.9 all-gather.8
  708.5 89.8 reduce-scatter.1
where the time goes:
time: 817 us; the launch traced here: 815 us
  waiting for transfers between devices  669 us (82%)
  matrix products  55 us (7%)
  blocking collectives  53.9 us (7%)
  between operations  13.9 us (2%)
  local copies, waits for them, and re-layouts  11.9 us (1%)
  other arithmetic  11.8 us (1%)
    all_gather x1, waiting for transfers between devices, refresh(): lax.all_gather(up_weight, 'group', axis=0, tiled=True)  179 us
    all_gather x1, waiting for transfers between devices, refresh(): lax.all_gather(gate_weight, 'group', axis=0, tiled=True)  170 us
    all_gather x1, waiting for transfers between devices, refresh(): lax.all_gather(down_weight, 'group', axis=1, tiled=True)  163 us
    reduce_scatter x1, waiting for transfers between devices, refresh(): lax.psum_scatter(partial_value.astype(jnp.bfloat16), 'mp', scatter_dimens...  83.8 us
    all_gather x1, waiting for transfers between devices, refresh(): full_rows = lax.all_gather(slots, 'mp', axis=2, tiled=True)  69.6 us
    all_to_all x1, blocking collectives, body(): lax.all_to_all(tokens, 'mp', split_axis=1, concat_axis=0, tiled=True)  53.9 us
    dot_general x1, matrix products, refresh(): jnp.dot(hidden, lax.all_gather(down_weight, 'group', axis=1, tiled=True),...  29.4 us
  transfers between devices with their start and end apart: 5, of which 5 were waited for; matrix products, arithmetic and copies ran while one was open for 3% of the time, Pallas kernels for 0%

commit v1 on v0

v1 whole, which is shorter than its diff:
```python
import jax
import jax.numpy as jnp
from jax import lax
from jax.sharding import PartitionSpec as P

BLK = 128


epsilon = 1e-05


def body(
    tokens,
    cached_update,
    norm_gain,
    gate_weight,
    up_weight,
    down_weight,
    stale_blocks,
    stale_count,
    lengths,
):
    n_group = lax.axis_size("group")
    n_mp = lax.axis_size("mp")
    split = n_mp // n_group
    group_id = lax.axis_index("group")
    mp_id = lax.axis_index("mp")
    group_ids = jnp.arange(n_group, dtype=jnp.int32)

    values = tokens.astype(jnp.float32)
    mean_sq = jnp.mean(values * values, axis=-1)
    all_mean_sq = lax.all_gather(mean_sq, "mp", axis=0, tiled=True)

    columns = lax.all_to_all(tokens, "mp", split_axis=1, concat_axis=0, tiled=True)
    seq_rows, col_width = columns.shape
    block_total = seq_rows // BLK
    column_blocks = columns.reshape(block_total, BLK, col_width)
    block_ids = jnp.arange(block_total, dtype=jnp.int32)

    count_before = jnp.sum(jnp.where(group_ids < group_id, stale_count, 0))
    own_count = jnp.sum(jnp.where(group_ids == group_id, stale_count, 0))
    own_list = stale_blocks[0]
    positions = jnp.arange(own_list.shape[0], dtype=jnp.int32)
    slot_of = jnp.where(positions < own_count, count_before + positions, -1)
    slots = jnp.arange(n_group, dtype=jnp.int32)
    slot_hits = slot_of[None, :] == slots[:, None]
    slot_block = jnp.sum(jnp.where(slot_hits, own_list[None, :], 0), axis=1)
    slot_own = jnp.any(slot_hits, axis=1)

    scale = lax.rsqrt(all_mean_sq + epsilon).reshape(block_total, BLK)
    own_gain = lax.dynamic_slice_in_dim(norm_gain, mp_id * col_width, col_width)
    placed = []
    for s in range(n_group):
        rows = lax.dynamic_index_in_dim(column_blocks, slot_block[s], 0, keepdims=False)
        row_scale = lax.dynamic_index_in_dim(scale, slot_block[s], 0, keepdims=False)
        normed = rows.astype(jnp.float32) * row_scale[:, None] * own_gain
        placed.append(jnp.where(slot_own[s], normed, 0.0).astype(jnp.bfloat16))
    placed = jnp.stack(placed)
    slot_rows = lax.psum_scatter(placed, "group", scatter_dimension=0, tiled=True)[0]

    pairs = [
        (s * n_mp + m, (m // split) * n_mp + s * split + m % split)
        for s in range(n_group)
        for m in range(n_mp)
    ]
    chunk_rows = lax.ppermute(slot_rows, ("group", "mp"), pairs)
    gathered = lax.all_gather(chunk_rows, "mp", axis=0)
    gathered = gathered.reshape(n_group, split, BLK, col_width)
    normed = gathered.transpose(0, 2, 1, 3).reshape(n_group * BLK, split * col_width)

    gate_part = jnp.dot(normed, gate_weight, preferred_element_type=jnp.float32)
    up_part = jnp.dot(normed, up_weight, preferred_element_type=jnp.float32)
    gate_vals = lax.psum_scatter(
        gate_part.astype(jnp.bfloat16), "group", scatter_dimension=0, tiled=True
    ).astype(jnp.float32)
    up_vals = lax.psum_scatter(
        up_part.astype(jnp.bfloat16), "group", scatter_dimension=0, tiled=True
    ).astype(jnp.float32)
    hidden = (jax.nn.silu(gate_vals) * up_vals).astype(jnp.bfloat16)
    hidden = lax.all_gather(hidden, "group", axis=0, tiled=True)

    partial_value = jnp.dot(hidden, down_weight, preferred_element_type=jnp.float32)
    partial_value = partial_value.astype(jnp.bfloat16)
    pieces = partial_value.reshape(n_group, BLK, split, col_width).transpose(0, 2, 1, 3)
    pieces = pieces.reshape(n_group * split, BLK, col_width)
    piece = lax.psum_scatter(pieces, "mp", scatter_dimension=0, tiled=True)[0]
    piece = lax.ppermute(piece, ("group", "mp"), [(b, a) for a, b in pairs])
    update = lax.all_gather(piece, "group", axis=0)

    listed = (own_list[None, :] == block_ids[:, None]) & (positions < own_count)[None, :]
    stale = jnp.any(listed, axis=1)
    block_slot = jnp.sum(jnp.where(listed, slot_of[None, :], 0), axis=1)
    cache_blocks = cached_update.reshape(block_total, BLK, col_width)
    outs = []
    for b in range(block_total):
        fresh = lax.dynamic_index_in_dim(update, block_slot[b], 0, keepdims=False)
        merged = jnp.where(stale[b], fresh, cache_blocks[b]).astype(jnp.float32)
        live = b * BLK + jnp.arange(BLK, dtype=jnp.int32) < lengths[0]
        total = column_blocks[b].astype(jnp.float32) + merged
        outs.append(jnp.where(live[:, None], total, 0.0).astype(jnp.bfloat16))
    return jnp.concatenate(outs, axis=0)


def solution(mesh):
    in_specs = (
        P(("group", "mp"), None),
        P("group", "mp"),
        P(),
        P("group", "mp"),
        P("group", "mp"),
        P("mp", "group"),
        P("group", None),
        P(),
        P("group"),
    )
    out_specs = P("group", "mp")
    return jax.shard_map(body, mesh=mesh, in_specs=in_specs, out_specs=out_specs, check_vma=False)
```

time: 817 us -> 452 us (0.55)
  waiting for transfers between devices: 669 us -> 246 us
  local copies, waits for them, and re-layouts: 11.9 us -> 62.8 us
  matrix products: 55 us -> 26 us
  between operations: 13.9 us -> 37.1 us
  blocking collectives: 53.9 us -> 37.2 us
  starting transfers between devices: 0.34 us -> 15.1 us
  other arithmetic: 11.8 us -> 25.2 us
    all_gather x4 -> x3, waiting for transfers between devices: 583 us -> 70.8 us  [the longest x1 49.7 us: body(): gathered = lax.all_gather(chunk_rows, 'mp', axis=0)]
    reduce_scatter x1 -> x4, waiting for transfers between devices: 83.8 us -> 149 us  [the longest x1 70 us: body(): piece = lax.psum_scatter(pieces, 'mp', scatter_dimension=0, tiled=True)[0]]
    all_to_all x1 -> x0, blocking collectives: 53.9 us -> none  [body(): lax.all_to_all(tokens, 'mp', split_axis=1, concat_axis=0, tiled=True)]
    all_gather x0 -> x1, blocking collectives: none -> 37.2 us  [body(): all_mean_sq = lax.all_gather(mean_sq, 'mp', axis=0, tiled=True)]
    dot_general x4 -> x3, matrix products: 55 us -> 26 us  [the longest x1 8.92 us: body(): jnp.dot(hidden, down_weight, preferred_element_type=jnp.float32)]
    ppermute x0 -> x2, waiting for transfers between devices: none -> 26.2 us  [the longest x1 13.3 us: body(): piece = lax.ppermute(piece, ('group', 'mp'), [(b, a) for a, b in pairs])]
    unnamed x15 -> x42, local copies, waits for them, and re-layouts: 5.59 us -> 29.6 us
    reshape x0 -> x4, local copies, waits for them, and re-layouts: none -> 21 us  [the longest x2 13 us: body(): gathered = gathered.reshape(n_group, split, BLK, col_width)]
  transfers between devices with their start and end apart: 5 -> 10, of which waited for: 5 -> 8; matrix products, arithmetic and copies ran while one was open for 3% -> 6% of each run, Pallas kernels for 0% -> 0%
where the time goes in v1:
time: 452 us; the launch traced here: 450 us
  waiting for transfers between devices  246 us (54%)
  local copies, waits for them, and re-layouts  62.8 us (14%)
  blocking collectives  37.2 us (8%)
  between operations  37.1 us (8%)
  matrix products  26 us (6%)
  other arithmetic  25.2 us (6%)
  starting transfers between devices  15.1 us (3%)
    reduce_scatter x1, waiting for transfers between devices, body(): piece = lax.psum_scatter(pieces, 'mp', scatter_dimension=0, tiled=True)[0]  70 us
    all_gather x1, waiting for transfers between devices, body(): gathered = lax.all_gather(chunk_rows, 'mp', axis=0)  49.7 us
    all_gather x1, blocking collectives, body(): all_mean_sq = lax.all_gather(mean_sq, 'mp', axis=0, tiled=True)  37.2 us
    reduce_scatter x1, waiting for transfers between devices, body(): lax.psum_scatter(up_part.astype(jnp.bfloat16), 'group', scatter_dimension...  32 us
    reduce_scatter x1, waiting for transfers between devices, body(): lax.psum_scatter(placed, 'group', scatter_dimension=0, tiled=True)[0]  29.6 us
    unnamed x42, local copies, waits for them, and re-layouts  29.6 us
    all_gather x1, waiting for transfers between devices, body(): hidden = lax.all_gather(hidden, 'group', axis=0, tiled=True)  21 us
    reduce_scatter x1, waiting for transfers between devices, body(): lax.psum_scatter(gate_part.astype(jnp.bfloat16), 'group', scatter_dimensi...  17.8 us
  transfers between devices with their start and end apart: 10, of which 8 were waited for; matrix products, arithmetic and copies ran while one was open for 6% of the time, Pallas kernels for 0%

profile of v1, /device:TPU:2, one launch (start us, length us, event | category | flops | bytes accessed | tf_op | source)
XLA Modules:
  0.0 449.9 jit_solution(11254690404291604662)
XLA Ops:
  6.5 4.1 copy.50
  10.6 6.0 %all-to-all-start = ((bf16[128,8,1024]{0,2,1:T(8,128)(2,1)}), bf16[128,8,1024]{0,2,1:T(8,128)(2,1)S(1)}, u32[]{:S(2)}, u32[]{:S(2)}) async-start(bf16[128,8,1024]{0,2,1:T(8,128)(2,1)} %bitcast.152), calls=%async_computation | async-start | bytes 4194304 | tf_op jit(solution)/shard_map/all_to_all | solution.py:34
  17.3 1.2 add_select_fusion
  26.8 2.1 multiply_reduce_fusion
  28.9 37.2 %all-gather.2 = f32[8,1,128]{2,1,0:T(1,128)S(1)} all-gather(f32[1,1,128]{2,1,0:T(1,128)S(1)} %multiply_bitcast_fusion), channel_id=1, replica_groups=mesh['group'=4,'mp'=8] {'mp'}, dimensions={0}, use_global_device_ids=true | all-gather | bytes 4608 | tf_op jit(solution)/shard_map/all_gather | solution.py:32
  67.0 2.8 fusion.30
  70.9 29.6 %reduce-scatter.5.cloned.1.call-done = bf16[1,128,1024]{1,2,0:T(8,128)(2,1)} async-done(((bf16[4,128,1024]{1,2,0:T(8,128)(2,1)}), bf16[1,128,1024]{1,2,0:T(8,128)(2,1)}) %reduce-scatter.5.cloned.1.call-update) | async-done | bytes 262160 | tf_op jit(solution)/shard_map/reduce_scatter | solution.py:59
  100.5 5.4 %collective-permute-start = (bf16[128,1024]{0,1:T(8,128)(2,1)}, bf16[128,1024]{0,1:T(8,128)(2,1)S(1)}, u32[]{:S(2)}, u32[]{:S(2)}) collective-permute-start(bf16[128,1024]{0,1:T(8,128)(2,1)} %bitcast.161), channel_id=1, source_target_pairs={{0,0},{1,1},{2,8},{3,9},{4,16},{5,17},{6,24},{7,25},{8,2},{9,3},{1... | collective-permute-start | bytes 786440 | tf_op jit(solution)/shard_map/ppermute | solution.py:66
  105.9 12.9 %collective-permute-done = bf16[128,1024]{0,1:T(8,128)(2,1)S(1)} collective-permute-done((bf16[128,1024]{0,1:T(8,128)(2,1)}, bf16[128,1024]{0,1:T(8,128)(2,1)S(1)}, u32[]{:S(2)}, u32[]{:S(2)}) %collective-permute-start) | collective-permute-done | bytes 262176 | tf_op jit(solution)/shard_map/ppermute | solution.py:66
  119.6 49.7 %all-gather.9.cloned.1.call-done = bf16[1024,1024]{0,1:T(8,128)(2,1)} async-done(((bf16[128,1024]{0,1:T(8,128)(2,1)}), bf16[1024,1024]{0,1:T(8,128)(2,1)}) %all-gather.9.cloned.1.call-update) | async-done | bytes 2097168 | tf_op jit(solution)/shard_map/all_gather | solution.py:67
  169.4 4.4 reshape.387
  173.8 8.5 %copy.52 = bf16[4,2,128,1024]{3,1,2,0:T(2,128)(2,1)} copy(bf16[4,2,128,1024]{2,1,0,3:T(2,128)(2,1)} %reshape.387) | data formatting | bytes 4194304 | tf_op jit(solution)/shard_map/reshape | solution.py:68
  182.3 2.2 copy.92
  184.6 1.3 copy-done
  185.9 8.2 %convolution_convert_fusion.2 = bf16[512,1792]{1,0:T(8,128)(2,1)} fusion(bf16[512,2048]{1,0:T(8,128)(2,1)S(1)} %bitcast.156, bf16[2048,1792]{1,0:T(8,128)(2,1)} %param.12), kind=kOutput, calls=%fused_computation.3 | convolution fusion | flops 3759013888 | bytes 11272192 | tf_op jit(solution)/shard_map/dot_general | solution.py:71
  194.1 8.9 %convolution_convert_fusion.1 = bf16[512,1792]{1,0:T(8,128)(2,1)} fusion(bf16[512,2048]{1,0:T(8,128)(2,1)} %bitcast.157, bf16[2048,1792]{1,0:T(8,128)(2,1)} %param.13), kind=kOutput, calls=%fused_computation.2 | convolution fusion | flops 3759013888 | bytes 11272192 | tf_op jit(solution)/shard_map/dot_general | solution.py:72
  203.1 17.8 %reduce-scatter.7.cloned.1.call-done = bf16[128,1792]{1,0:T(8,128)(2,1)} async-done(((bf16[512,1792]{1,0:T(8,128)(2,1)}), bf16[128,1792]{1,0:T(8,128)(2,1)}) %reduce-scatter.7.cloned.1.call-update) | async-done | bytes 458768 | tf_op jit(solution)/shard_map/reduce_scatter | solution.py:73
  220.9 32.0 %reduce-scatter.9.cloned.1.call-done = bf16[128,1792]{1,0:T(8,128)(2,1)} async-done(((bf16[512,1792]{1,0:T(8,128)(2,1)}), bf16[128,1792]{1,0:T(8,128)(2,1)}) %reduce-scatter.9.cloned.1.call-update) | async-done | bytes 458768 | tf_op jit(solution)/shard_map/reduce_scatter | solution.py:76
  252.9 2.2 fusion.4
  255.4 21.0 %all-gather.7.cloned.1.call-done = bf16[512,1792]{1,0:T(8,128)(2,1)} async-done(((bf16[128,1792]{1,0:T(8,128)(2,1)}), bf16[512,1792]{1,0:T(8,128)(2,1)}) %all-gather.7.cloned.1.call-update) | async-done | bytes 1835024 | tf_op jit(solution)/shard_map/all_gather | solution.py:80
  276.4 8.9 %convolution_convert_fusion = bf16[512,2048]{1,0:T(8,128)(2,1)} fusion(bf16[512,1792]{1,0:T(8,128)(2,1)} %all-gather.7.cloned.1.call-done, bf16[1792,2048]{1,0:T(8,128)(2,1)} %param.14), kind=kOutput, calls=%fused_computation.1 | convolution fusion | flops 3759144960 | bytes 11272192 | tf_op jit(solution)/shard_map/dot_general | solution.py:82
  285.3 4.5 %reshape.389 = bf16[4,128,2,1024]{3,2,1,0:T(2,128)(2,1)} reshape(bf16[512,2048]{1,0:T(8,128)(2,1)} %convolution_convert_fusion) | data formatting | bytes 4194304 | tf_op jit(solution)/shard_map/reshape | solution.py:84
  289.8 3.5 copy.53
  293.4 70.0 %reduce-scatter.11.cloned.1.call-done = bf16[1,128,1024]{2,1,0:T(8,128)(2,1)} async-done(((bf16[8,128,1024]{2,1,0:T(8,128)(2,1)}), bf16[1,128,1024]{2,1,0:T(8,128)(2,1)}) %reduce-scatter.11.cloned.1.call-update) | async-done | bytes 262160 | tf_op jit(solution)/shard_map/reduce_scatter | solution.py:86
  363.4 3.2 collective-permute-start.1
  366.6 13.3 %collective-permute-done.1 = bf16[128,1024]{1,0:T(8,128)(2,1)S(1)} collective-permute-done((bf16[128,1024]{1,0:T(8,128)(2,1)}, bf16[128,1024]{1,0:T(8,128)(2,1)S(1)}, u32[]{:S(2)}, u32[]{:S(2)}) %collective-permute-start.1) | collective-permute-done | bytes 262176 | tf_op jit(solution)/shard_map/ppermute | solution.py:87
  392.2 2.5 fusion.49
  394.7 1.8 copy.77
  397.2 1.8 copy.79
  400.5 1.1 copy.91
  407.6 3.1 constant_dynamic-slice_fusion
  410.6 1.8 copy.76
  412.4 1.8 copy.78
  414.2 1.8 copy.80
  416.0 1.8 copy.82
  417.8 1.8 copy.84
  419.6 1.8 copy.86
  421.4 1.8 copy.88
  423.2 1.8 copy.90
  425.0 2.6 fusion.33
  427.6 2.4 fusion.34
  430.1 1.6 fusion.35
  431.7 1.5 fusion.36
  433.2 1.6 fusion.37
  434.7 1.5 fusion.38
  436.2 1.5 fusion.39
  437.7 1.5 fusion.40
  439.1 3.9 copy.70
  (64 shorter events, 9.0 us)
Async XLA Ops:
  10.6 6.0 %copy-start.10 = (s32[4]{0:T(128)S(1)}, s32[4]{0:T(128)}, u32[]{:S(2)}) copy-start(s32[4]{0:T(128)} %param.16) | copy-start | bytes 52
  10.6 8.0 %copy-start.11 = (s32[1,2]{1,0:T(1,128)S(1)}, s32[1,2]{1,0:T(1,128)}, u32[]{:S(2)}) copy-start(s32[1,2]{1,0:T(1,128)} %param.15) | copy-start | bytes 28
  10.6 56.3 %all-to-all-start = ((bf16[128,8,1024]{0,2,1:T(8,128)(2,1)}), bf16[128,8,1024]{0,2,1:T(8,128)(2,1)S(1)}, u32[]{:S(2)}, u32[]{:S(2)}) async-start(bf16[128,8,1024]{0,2,1:T(8,128)(2,1)} %bitcast.152), calls=%async_computation | async-start | bytes 4194304 | tf_op jit(solution)/shard_map/all_to_all | solution.py:34
  16.6 83.9 %reduce-scatter.5.cloned.1.call-start = ((), (), s32[]{:S(2)}) async-start(), calls=%async_computation.5 | async-start | bytes 1310720 | tf_op jit(solution)/shard_map/reduce_scatter | solution.py:59
  26.8 40.1 %dynamic-slice-start = ((f32[8192]{0:T(1024)}, s32[]{:T(128)}), f32[1024]{0:T(1024)S(1)}, s32[]{:S(2)}) async-start(f32[8192]{0:T(1024)} %param.11, s32[]{:T(128)} %select_n.205), calls=%async_computation.12 | async-start | bytes 8704 | tf_op jit(solution)/shard_map/dynamic_slice | solution.py:51
  70.9 98.5 %all-gather.9.cloned.1.call-start = ((), (), s32[]{:S(2)}) async-start(), calls=%async_computation.10 | async-start | bytes 2359296 | tf_op jit(solution)/shard_map/all_gather | solution.py:67
  100.5 18.4 %collective-permute-start = (bf16[128,1024]{0,1:T(8,128)(2,1)}, bf16[128,1024]{0,1:T(8,128)(2,1)S(1)}, u32[]{:S(2)}, u32[]{:S(2)}) collective-permute-start(bf16[128,1024]{0,1:T(8,128)(2,1)} %bitcast.161), channel_id=1, source_target_pairs={{0,0},{1,1},{2,8},{3,9},{4,16},{5,17},{6,24},{7,25},{8,2},{9,3},{1... | collective-permute-start | bytes 786440 | tf_op jit(solution)/shard_map/ppermute | solution.py:66
  118.9 0.7 copy-start.9
  119.6 101.3 %reduce-scatter.7.cloned.1.call-start = ((), (), s32[]{:S(2)}) async-start(), calls=%async_computation.6 | async-start | bytes 2293760 | tf_op jit(solution)/shard_map/reduce_scatter | solution.py:73
  184.5 1.3 copy-start
  194.1 58.8 %reduce-scatter.9.cloned.1.call-start = ((), (), s32[]{:S(2)}) async-start(), calls=%async_computation.7 | async-start | bytes 2293760 | tf_op jit(solution)/shard_map/reduce_scatter | solution.py:76
  203.0 73.3 %all-gather.7.cloned.1.call-start = ((), (), s32[]{:S(2)}) async-start(), calls=%async_computation.8 | async-start | bytes 2293760 | tf_op jit(solution)/shard_map/all_gather | solution.py:80
  255.1 108.3 %reduce-scatter.11.cloned.1.call-start = ((), (), s32[]{:S(2)}) async-start(), calls=%async_computation.9 | async-start | bytes 2359296 | tf_op jit(solution)/shard_map/reduce_scatter | solution.py:86
  293.4 114.2 %all-gather.11.cloned.1.call-start = ((), (), s32[]{:S(2)}) async-start(), calls=%async_computation.11 | async-start | bytes 1310720 | tf_op jit(solution)/shard_map/all_gather | solution.py:88
  363.4 16.5 %collective-permute-start.1 = (bf16[128,1024]{1,0:T(8,128)(2,1)}, bf16[128,1024]{1,0:T(8,128)(2,1)S(1)}, u32[]{:S(2)}, u32[]{:S(2)}) collective-permute-start(bf16[128,1024]{1,0:T(8,128)(2,1)} %bitcast.162), channel_id=1, source_target_pairs={{0,0},{1,1},{8,2},{9,3},{16,4},{17,5},{24,6},{25,7},{2,8},{3,9},{1... | collective-permute-start | bytes 786440 | tf_op jit(solution)/shard_map/ppermute | solution.py:87
  379.9 0.7 copy-start.8
  425.0 5.1 %copy-start.1 = (bf16[128,1024]{0,1:T(8,128)(2,1)S(1)}, bf16[128,1024]{0,1:T(8,128)(2,1)}, u32[]{:S(2)}) copy-start(bf16[128,1024]{0,1:T(8,128)(2,1)} %copy.81) | copy-start | bytes 786436
  425.0 5.1 %copy-start.7 = (bf16[1,128,1024]{1,2,0:T(8,128)(2,1)S(1)}, bf16[1,128,1024]{1,2,0:T(8,128)(2,1)}, u32[]{:S(2)}) copy-start(bf16[1,128,1024]{1,2,0:T(8,128)(2,1)} %copy.80) | copy-start | bytes 786436
  425.0 6.7 %copy-start.6 = (bf16[1,128,1024]{1,2,0:T(8,128)(2,1)S(1)}, bf16[1,128,1024]{1,2,0:T(8,128)(2,1)}, u32[]{:S(2)}) copy-start(bf16[1,128,1024]{1,2,0:T(8,128)(2,1)} %copy.82) | copy-start | bytes 786436
  425.0 8.2 %copy-start.5 = (bf16[1,128,1024]{1,2,0:T(8,128)(2,1)S(1)}, bf16[1,128,1024]{1,2,0:T(8,128)(2,1)}, u32[]{:S(2)}) copy-start(bf16[1,128,1024]{1,2,0:T(8,128)(2,1)} %copy.84) | copy-start | bytes 786436
  427.6 7.1 %copy-start.4 = (bf16[1,128,1024]{1,2,0:T(8,128)(2,1)S(1)}, bf16[1,128,1024]{1,2,0:T(8,128)(2,1)}, u32[]{:S(2)}) copy-start(bf16[1,128,1024]{1,2,0:T(8,128)(2,1)} %copy.86) | copy-start | bytes 786436
  430.1 6.1 %copy-start.3 = (bf16[1,128,1024]{1,2,0:T(8,128)(2,1)S(1)}, bf16[1,128,1024]{1,2,0:T(8,128)(2,1)}, u32[]{:S(2)}) copy-start(bf16[1,128,1024]{1,2,0:T(8,128)(2,1)} %copy.88) | copy-start | bytes 786436
  431.7 6.0 %copy-start.2 = (bf16[1,128,1024]{1,2,0:T(8,128)(2,1)S(1)}, bf16[1,128,1024]{1,2,0:T(8,128)(2,1)}, u32[]{:S(2)}) copy-start(bf16[1,128,1024]{1,2,0:T(8,128)(2,1)} %copy.90) | copy-start | bytes 786436
Sparse Core Ops, SparseCore 0:
  71.0 29.4 reduce-scatter.4
  119.7 49.6 all-gather.8
  194.2 26.6 reduce-scatter.6
  223.3 29.5 reduce-scatter.8
  255.2 21.0 all-gather.6
  293.5 69.8 reduce-scatter.10
  380.8 13.6 all-gather.10

commit v2 on v1

--- a/solution.py
+++ b/solution.py
@@ -1,12 +1,153 @@
+import functools
+
 import jax
 import jax.numpy as jnp
 from jax import lax
+from jax.experimental import pallas as pl
+from jax.experimental.pallas import tpu as pltpu
 from jax.sharding import PartitionSpec as P
 
 BLK = 128
 
 
 epsilon = 1e-05
+
+
+MESH = pl.DeviceIdType.MESH
+
+
+def enter(axis, peers):
+    barrier = pltpu.get_barrier_semaphore()
+    for peer in peers:
+        pl.semaphore_signal(barrier, inc=1, device_id={axis: peer}, device_id_type=MESH)
+    pl.semaphore_wait(barrier, len(peers))
+
+
+def swap_kernel(axis, n, count, *refs):
+    sources, targets, (send_sem, recv_sem) = refs[:count], refs[count : 2 * count], refs[2 * count :]
+    me = lax.axis_index(axis)
+    peers = [lax.rem(me + k, n) for k in range(1, n)]
+    enter(axis, peers)
+    copies = []
+    for k, peer in enumerate(peers):
+        for i in range(count):
+            copy = pltpu.make_async_remote_copy(
+                src_ref=sources[i].at[peer],
+                dst_ref=targets[i].at[k],
+                send_sem=send_sem.at[i, k],
+                recv_sem=recv_sem.at[i, k],
+                device_id={axis: peer},
+                device_id_type=MESH,
+            )
+            copy.start()
+            copies.append(copy)
+    for copy in copies:
+        copy.wait()
+
+
+def sum_scatter(arrays, axis, n, call_id):
+    count = len(arrays)
+    got = pl.pallas_call(
+        functools.partial(swap_kernel, axis, n, count),
+        out_shape=[jax.ShapeDtypeStruct((n - 1,) + a.shape[1:], a.dtype) for a in arrays],
+        in_specs=[pl.BlockSpec(memory_space=pl.ANY)] * count,
+        out_specs=[pl.BlockSpec(memory_space=pl.ANY)] * count,
+        scratch_shapes=[
+            pltpu.SemaphoreType.DMA((count, n - 1)),
+            pltpu.SemaphoreType.DMA((count, n - 1)),
+        ],
+        compiler_params=pltpu.CompilerParams(collective_id=call_id, has_side_effects=True),
+    )(*arrays)
+    me = lax.axis_index(axis)
+    sums = []
+    for array, parts in zip(arrays, got):
+        total = lax.dynamic_index_in_dim(array, me, 0, keepdims=False).astype(jnp.float32)
+        for k in range(n - 1):
+            total = total + parts[k].astype(jnp.float32)
+        sums.append(total)
+    return sums
+
+
+def spread_kernel(axis, n, x_ref, out_ref, own_sem, far_send, far_recv, near_send, near_recv):
+    me = lax.axis_index(axis)
+    far, near = lax.div(me, 2), lax.rem(me, 2)
+    n_far = n // 2
+    partner = far * 2 + (1 - near)
+    others = [lax.rem(far + k, n_far) * 2 + near for k in range(1, n_far)]
+    enter(axis, others + [partner])
+
+    def send(source, slot, send_sem, recv_sem, peer):
+        copy = pltpu.make_async_remote_copy(
+            src_ref=source,
+            dst_ref=out_ref.at[slot],
+            send_sem=send_sem,
+            recv_sem=recv_sem,
+            device_id={axis: peer},
+            device_id_type=MESH,
+        )
+        copy.start()
+        return copy
+
+    far_copies = [
+        send(x_ref, me, far_send.at[k], far_recv.at[k], peer) for k, peer in enumerate(others)
+    ]
+    near_copies = [send(x_ref, me, near_send.at[0], near_recv.at[0], partner)]
+    own = pltpu.make_async_copy(x_ref, out_ref.at[me], own_sem)
+    own.start()
+    for k in range(1, n_far):
+        far_copies[k - 1].wait_recv()
+        slot = lax.rem(far + (n_far - k), n_far) * 2 + near
+        near_copies.append(
+            send(out_ref.at[slot], slot, near_send.at[k], near_recv.at[k], partner)
+        )
+    own.wait()
+    for copy in far_copies:
+        copy.wait_send()
+    for copy in near_copies:
+        copy.wait()
+
+
+def gather(x, axis, n, call_id):
+    return pl.pallas_call(
+        functools.partial(spread_kernel, axis, n),
+        out_shape=jax.ShapeDtypeStruct((n,) + x.shape, x.dtype),
+        in_specs=[pl.BlockSpec(memory_space=pltpu.VMEM)],
+        out_specs=pl.BlockSpec(memory_space=pl.ANY),
+        scratch_shapes=[
+            pltpu.SemaphoreType.DMA,
+            pltpu.SemaphoreType.DMA((n // 2 - 1,)),
+            pltpu.SemaphoreType.DMA((n // 2 - 1,)),
+            pltpu.SemaphoreType.DMA((n // 2,)),
+            pltpu.SemaphoreType.DMA((n // 2,)),
+        ],
+        compiler_params=pltpu.CompilerParams(collective_id=call_id, has_side_effects=True),
+    )(x)
+
+
+def merge_kernel(slot_ref, stale_ref, length_ref, rows_ref, cache_ref, update_ref, out_ref):
+    b = pl.program_id(0)
+    fresh = update_ref[...].astype(jnp.float32)
+    cached = cache_ref[...].astype(jnp.float32)
+    merged = jnp.where(stale_ref[b] > 0, fresh, cached)
+    row = b * BLK + lax.broadcasted_iota(jnp.int32, out_ref.shape, 0)
+    total = rows_ref[...].astype(jnp.float32) + merged
+    out_ref[...] = jnp.where(row < length_ref[0], total, 0.0).astype(out_ref.dtype)
+
+
+def merge(columns, cached_update, update, block_slot, stale, lengths):
+    width = columns.shape[1]
+    block = pl.BlockSpec((BLK, width), lambda b, *_: (b, 0))
+    picked = pl.BlockSpec((None, BLK, width), lambda b, slot, *_: (slot[b], 0, 0))
+    return pl.pallas_call(
+        merge_kernel,
+        out_shape=jax.ShapeDtypeStruct(columns.shape, columns.dtype),
+        grid_spec=pltpu.PrefetchScalarGridSpec(
+            num_scalar_prefetch=3,
+            grid=(columns.shape[0] // BLK,),
+            in_specs=[block, block, picked],
+            out_specs=block,
+        ),
+    )(block_slot, stale, lengths, columns, cached_update, update)
 
 
 def body(
@@ -56,7 +197,7 @@
         normed = rows.astype(jnp.float32) * row_scale[:, None] * own_gain
         placed.append(jnp.where(slot_own[s], normed, 0.0).astype(jnp.bfloat16))
     placed = jnp.stack(placed)
-    slot_rows = lax.psum_scatter(placed, "group", scatter_dimension=0, tiled=True)[0]
+    slot_rows = sum_scatter([placed], "group", n_group, 0)[0].astype(jnp.bfloat16)
 
     pairs = [
         (s * n_mp + m, (m // split) * n_mp + s * split + m % split)
@@ -64,41 +205,32 @@
         for m in range(n_mp)
     ]
     chunk_rows = lax.ppermute(slot_rows, ("group", "mp"), pairs)
-    gathered = lax.all_gather(chunk_rows, "mp", axis=0)
+    gathered = gather(chunk_rows, "mp", n_mp, 1)
     gathered = gathered.reshape(n_group, split, BLK, col_width)
     normed = gathered.transpose(0, 2, 1, 3).reshape(n_group * BLK, split * col_width)
 
     gate_part = jnp.dot(normed, gate_weight, preferred_element_type=jnp.float32)
     up_part = jnp.dot(normed, up_weight, preferred_element_type=jnp.float32)
-    gate_vals = lax.psum_scatter(
-        gate_part.astype(jnp.bfloat16), "group", scatter_dimension=0, tiled=True
-    ).astype(jnp.float32)
-    up_vals = lax.psum_scatter(
-        up_part.astype(jnp.bfloat16), "group", scatter_dimension=0, tiled=True
-    ).astype(jnp.float32)
+    parts = [
+        part.astype(jnp.bfloat16).reshape(n_group, BLK, part.shape[1])
+        for part in (gate_part, up_part)
+    ]
+    gate_vals, up_vals = sum_scatter(parts, "group", n_group, 2)
     hidden = (jax.nn.silu(gate_vals) * up_vals).astype(jnp.bfloat16)
-    hidden = lax.all_gather(hidden, "group", axis=0, tiled=True)
+    hidden = gather(hidden, "group", n_group, 3).reshape(n_group * BLK, hidden.shape[1])
 
     partial_value = jnp.dot(hidden, down_weight, preferred_element_type=jnp.float32)
     partial_value = partial_value.astype(jnp.bfloat16)
     pieces = partial_value.reshape(n_group, BLK, split, col_width).transpose(0, 2, 1, 3)
     pieces = pieces.reshape(n_group * split, BLK, col_width)
-    piece = lax.psum_scatter(pieces, "mp", scatter_dimension=0, tiled=True)[0]
+    piece = sum_scatter([pieces], "mp", n_mp, 4)[0].astype(jnp.bfloat16)
     piece = lax.ppermute(piece, ("group", "mp"), [(b, a) for a, b in pairs])
-    update = lax.all_gather(piece, "group", axis=0)
+    update = gather(piece, "group", n_group, 5)
 
     listed = (own_list[None, :] == block_ids[:, None]) & (positions < own_count)[None, :]
     stale = jnp.any(listed, axis=1)
     block_slot = jnp.sum(jnp.where(listed, slot_of[None, :], 0), axis=1)
-    cache_blocks = cached_update.reshape(block_total, BLK, col_width)
-    outs = []
-    for b in range(block_total):
-        fresh = lax.dynamic_index_in_dim(update, block_slot[b], 0, keepdims=False)
-        merged = jnp.where(stale[b], fresh, cache_blocks[b]).astype(jnp.float32)
-        live = b * BLK + jnp.arange(BLK, dtype=jnp.int32) < lengths[0]
-        total = column_blocks[b].astype(jnp.float32) + merged
-        outs.append(jnp.where(live[:, None], total, 0.0).astype(jnp.bfloat16))
-    return jnp.concatenate(outs, axis=0)
+    return merge(columns, cached_update, update, block_slot, stale.astype(jnp.int32), lengths)
 
 
 def solution(mesh):

time: 452 us -> 320 us (0.71)
  waiting for transfers between devices: 246 us -> 21.6 us
  Pallas kernels: 0 us -> 159 us
  local copies, waits for them, and re-layouts: 62.8 us -> 18.2 us
  between operations: 37.1 us -> 8.15 us
  starting transfers between devices: 15.1 us -> 32 us
  other arithmetic: 25.2 us -> 16.7 us
    pallas_call x0 -> x7, Pallas kernels: none -> 159 us  [the longest x3 95.5 us: sum_scatter(): pl.pallas_call(functools.partial(swap_kernel, axis, n, count), out_shape=...]
    reduce_scatter x4 -> x0, waiting for transfers between devices: 149 us -> none  [the longest x1 70 us: body(): piece = lax.psum_scatter(pieces, 'mp', scatter_dimension=0, tiled=True)[0]]
    all_gather x3 -> x0, waiting for transfers between devices: 70.8 us -> none  [the longest x1 49.7 us: body(): gathered = lax.all_gather(chunk_rows, 'mp', axis=0)]
    unnamed x42 -> x16, local copies, waits for them, and re-layouts: 29.6 us -> 5.24 us
    unnamed x8 -> x2, other arithmetic: 12.7 us -> 0.01 us
    ppermute x1, starting transfers between devices: 3.21 us -> 13.9 us  [body(): piece = lax.ppermute(piece, ('group', 'mp'), [(b, a) for a, b in pairs])]
    reshape x2 -> x1, local copies, waits for them, and re-layouts: 13 us -> 3.75 us  [body(): gathered = gathered.reshape(n_group, split, BLK, col_width)]
    ppermute x1, starting transfers between devices: 5.43 us -> 12.1 us  [body(): chunk_rows = lax.ppermute(slot_rows, ('group', 'mp'), pairs)]
  transfers between devices with their start and end apart: 10 -> 3, of which waited for: 8 -> 2; matrix products, arithmetic and copies ran while one was open for 6% -> 2% of each run, Pallas kernels for 0% -> 0%
where the time goes in v2:
time: 320 us; the launch traced here: 316 us
  Pallas kernels  159 us (50%)
  blocking collectives  37.5 us (12%)
  starting transfers between devices  32 us (10%)
  matrix products  22.5 us (7%)
  waiting for transfers between devices  21.6 us (7%)
  local copies, waits for them, and re-layouts  18.2 us (6%)
  other arithmetic  16.7 us (5%)
  between operations  8.15 us (3%)
    pallas_call x3, Pallas kernels, sum_scatter(): pl.pallas_call(functools.partial(swap_kernel, axis, n, count), out_shape=...  95.5 us
    pallas_call x3, Pallas kernels, gather(): pl.pallas_call(functools.partial(spread_kernel, axis, n), out_shape=jax.S...  56.8 us
    all_gather x1, blocking collectives, body(): all_mean_sq = lax.all_gather(mean_sq, 'mp', axis=0, tiled=True)  37.5 us
    ppermute x1, starting transfers between devices, body(): piece = lax.ppermute(piece, ('group', 'mp'), [(b, a) for a, b in pairs])  13.9 us
    ppermute x1, waiting for transfers between devices, body(): chunk_rows = lax.ppermute(slot_rows, ('group', 'mp'), pairs)  12.6 us
    ppermute x1, starting transfers between devices, body(): chunk_rows = lax.ppermute(slot_rows, ('group', 'mp'), pairs)  12.1 us
    ppermute x1, waiting for transfers between devices, body(): piece = lax.ppermute(piece, ('group', 'mp'), [(b, a) for a, b in pairs])  8.98 us
    dot_general x1, matrix products, body(): jnp.dot(hidden, down_weight, preferred_element_type=jnp.float32)  8.92 us
  transfers between devices with their start and end apart: 3, of which 2 were waited for; matrix products, arithmetic and copies ran while one was open for 2% of the time, Pallas kernels for 0%

profile of v2, /device:TPU:2, one launch (start us, length us, event | category | flops | bytes accessed | tf_op | source)
XLA Modules:
  0.0 315.9 jit_solution(5428467793214164119)
XLA Ops:
  0.0 3.2 %copy.19 = bf16[128,8192]{0,1:T(8,128)(2,1)S(1)} copy(bf16[128,8192]{1,0:T(8,128)(2,1)} %param.9) | data formatting | bytes 4194304 | tf_op args[0]
  3.2 2.6 copy.20
  5.8 6.0 %all-to-all-start = ((bf16[128,8,1024]{2,0,1:T(8,128)(2,1)}), bf16[128,8,1024]{2,0,1:T(8,128)(2,1)S(1)}, u32[]{:S(2)}, u32[]{:S(2)}) async-start(bf16[128,8,1024]{2,0,1:T(8,128)(2,1)} %copy.20), calls=%async_computation | async-start | bytes 4194304 | tf_op jit(solution)/shard_map/all_to_all | solution.py:175
  11.8 0.0 copy-done.3
  11.8 0.7 fusion.21
  12.5 1.3 add_select_fusion
  13.8 0.0 copy-done.4
  13.8 0.1 select_reduce_fusion
  13.9 0.7 fusion.27
  21.8 0.0 dynamic-slice-start
  21.8 2.1 multiply_reduce_fusion
  23.9 37.5 %all-gather = f32[8,1,128]{2,1,0:T(1,128)S(1)} all-gather(f32[1,1,128]{2,1,0:T(1,128)S(1)} %multiply_bitcast_fusion), channel_id=1, replica_groups=mesh['group'=4,'mp'=8] {'mp'}, dimensions={0}, use_global_device_ids=true | all-gather | bytes 4608 | tf_op jit(solution)/shard_map/all_gather | solution.py:173
  61.4 0.1 fusion.18
  61.5 0.7 fusion.26
  62.2 0.0 all-to-all-done
  62.2 0.0 dynamic-slice-done
  62.2 2.8 fusion.15
  65.0 1.1 pad_maximum_fusion.refs_0_
  66.1 0.0 copy-done
  66.1 12.6 %shard_map.91 = bf16[3,128,1024]{2,1,0:T(8,128)(2,1)} custom-call(bf16[4,128,1024]{2,1,0:T(8,128)(2,1)} %pad_maximum_fusion.refs_0_), custom_call_target="tpu_custom_call" | custom-call | tf_op jit(solution)/shard_map/pallas_call | solution.py:50
  78.7 1.4 fusion.16
  80.1 12.1 %collective-permute-start = (bf16[128,1024]{1,0:T(8,128)(2,1)S(1)}, bf16[128,1024]{1,0:T(8,128)(2,1)S(1)}, u32[]{:S(2)}, u32[]{:S(2)}) collective-permute-start(bf16[128,1024]{1,0:T(8,128)(2,1)S(1)} %fusion.16), channel_id=1, source_target_pairs={{0,0},{1,1},{2,8},{3,9},{4,16},{5,17},{6,24},{7,25},{8,2},{9,3},{1... | collective-permute-start | bytes 786440 | tf_op jit(solution)/shard_map/ppermute | solution.py:207
  92.2 12.6 %collective-permute-done.x_ref = bf16[128,1024]{1,0:T(8,128)(2,1)S(1)} collective-permute-done((bf16[128,1024]{1,0:T(8,128)(2,1)S(1)}, bf16[128,1024]{1,0:T(8,128)(2,1)S(1)}, u32[]{:S(2)}, u32[]{:S(2)}) %collective-permute-start) | collective-permute-done | bytes 262176 | tf_op jit(solution)/shard_map/ppermute | solution.py:207
  104.8 0.7 copy-done.2
  105.5 31.7 %shard_map.92 = bf16[8,128,1024]{2,1,0:T(8,128)(2,1)} custom-call(bf16[128,1024]{1,0:T(8,128)(2,1)} %copy-done.2), custom_call_target="tpu_custom_call" | custom-call | tf_op jit(solution)/shard_map/pallas_call | solution.py:111
  137.3 3.7 %copy.22 = bf16[4,2,128,1024]{3,1,2,0:T(2,128)(2,1)S(1)} copy(bf16[4,2,128,1024]{3,2,1,0:T(8,128)(2,1)} %bitcast.76) | data formatting | bytes 4194304 | tf_op jit(solution)/shard_map/reshape | solution.py:209
  141.0 0.0 slice-start
  141.0 0.6 copy.29
  141.6 0.0 slice-start.1
  141.6 8.5 %convolution_convert_fusion.2 = bf16[512,1792]{1,0:T(8,128)(2,1)} fusion(bf16[512,2048]{1,0:T(8,128)(2,1)S(1)} %bitcast.83, bf16[2048,1792]{1,0:T(8,128)(2,1)} %param.12), kind=kOutput, calls=%fused_computation.3 | convolution fusion | flops 3759013888 | bytes 11272192 | tf_op jit(solution)/shard_map/dot_general | solution.py:212
  150.1 5.1 %convolution_convert_fusion.1 = bf16[512,1792]{1,0:T(8,128)(2,1)} fusion(bf16[512,2048]{1,0:T(8,128)(2,1)S(1)} %bitcast.84, bf16[2048,1792]{1,0:T(8,128)(2,1)S(1)} %bitcast.90), kind=kOutput, calls=%fused_computation.2 | convolution fusion | flops 3759013888 | bytes 11272192 | tf_op jit(solution)/shard_map/dot_general | solution.py:213
  155.2 42.6 %shard_map.93 = (bf16[3,128,1792]{2,1,0:T(8,128)(2,1)}, bf16[3,128,1792]{2,1,0:T(8,128)(2,1)}) custom-call(bf16[4,128,1792]{2,1,0:T(8,128)(2,1)} %bitcast.79, bf16[4,128,1792]{2,1,0:T(8,128)(2,1)} %bitcast.81), custom_call_target="tpu_custom_call" | custom-call | tf_op jit(solution)/shard_map/pallas_call | solution.py:50
  197.8 3.4 %fusion.x_ref = bf16[128,1792]{1,0:T(8,128)(2,1)} fusion(bf16[3,128,1792]{2,1,0:T(8,128)(2,1)} %get-tuple-element.8, bf16[4,128,1792]{2,1,0:T(8,128)(2,1)} %bitcast.82, s32[]{:T(128)S(6)} %select_n.126, bf16[3,128,1792]{2,1,0:T(8,128)(2,1)} %get-tuple-element.7, bf16[4,128,1792]{2,1,0:T(8,128)(2,1)} %bitcast.80), kind=kLoop, calls=%fused_computation.6 | loop fusion | flops 4587520 | bytes 4128772 | tf_op jit(solution)/shard_map/convert_element_type | solution.py:219
  201.2 16.1 %shard_map.94 = bf16[4,128,1792]{2,1,0:T(8,128)(2,1)} custom-call(bf16[128,1792]{1,0:T(8,128)(2,1)} %fusion.x_ref), custom_call_target="tpu_custom_call" | custom-call | tf_op jit(solution)/shard_map/pallas_call | solution.py:111
  217.3 8.9 %convolution_convert_fusion = bf16[512,2048]{1,0:T(8,128)(2,1)} fusion(bf16[512,1792]{1,0:T(8,128)(2,1)} %bitcast.85, bf16[1792,2048]{1,0:T(8,128)(2,1)} %param.14), kind=kOutput, calls=%fused_computation.1 | convolution fusion | flops 3759144960 | bytes 11272192 | tf_op jit(solution)/shard_map/dot_general | solution.py:222
  226.2 3.3 %reshape.366 = bf16[4,128,2,1024]{3,2,1,0:T(2,128)(2,1)S(1)} reshape(bf16[512,2048]{1,0:T(8,128)(2,1)} %convolution_convert_fusion) | data formatting | bytes 4194304 | tf_op jit(solution)/shard_map/reshape | solution.py:224
  229.5 2.0 copy.23
  231.4 40.3 %shard_map.95 = bf16[7,128,1024]{2,1,0:T(8,128)(2,1)} custom-call(bf16[8,128,1024]{2,1,0:T(8,128)(2,1)} %bitcast.74), custom_call_target="tpu_custom_call" | custom-call | tf_op jit(solution)/shard_map/pallas_call | solution.py:50
  271.7 1.9 fusion.17
  273.6 13.9 %collective-permute-start.1 = (bf16[128,1024]{1,0:T(8,128)(2,1)S(1)}, bf16[128,1024]{1,0:T(8,128)(2,1)S(1)}, u32[]{:S(2)}, u32[]{:S(2)}) collective-permute-start(bf16[128,1024]{1,0:T(8,128)(2,1)S(1)} %fusion.17), channel_id=1, source_target_pairs={{0,0},{1,1},{8,2},{9,3},{16,4},{17,5},{24,6},{25,7},{2,8},{3,9},{1... | collective-permute-start | bytes 786440 | tf_op jit(solution)/shard_map/ppermute | solution.py:227
  287.5 0.7 iota_compare_fusion.1
  288.2 0.1 fusion.19
  288.3 0.6 convert_element_type.202.stale_ref
  289.5 0.6 select_reduce_fusion.1.slot_ref
  290.1 9.0 %collective-permute-done.1.x_ref = bf16[128,1024]{1,0:T(8,128)(2,1)S(1)} collective-permute-done((bf16[128,1024]{1,0:T(8,128)(2,1)S(1)}, bf16[128,1024]{1,0:T(8,128)(2,1)S(1)}, u32[]{:S(2)}, u32[]{:S(2)}) %collective-permute-start.1) | collective-permute-done | bytes 262176 | tf_op jit(solution)/shard_map/ppermute | solution.py:227
  299.1 0.7 copy-done.1
  299.8 9.0 %shard_map.96.update_ref = bf16[4,128,1024]{2,1,0:T(8,128)(2,1)} custom-call(bf16[128,1024]{1,0:T(8,128)(2,1)} %copy-done.1), custom_call_target="tpu_custom_call" | custom-call | tf_op jit(solution)/shard_map/pallas_call | solution.py:111
  308.8 7.1 %shard_map.97 = bf16[1024,1024]{1,0:T(8,128)(2,1)} custom-call(s32[8]{0:T(128)} %select_reduce_fusion.1.slot_ref, s32[8]{0:T(128)} %convert_element_type.202.stale_ref, s32[1]{0:T(128)S(6)} %copy.30.length_ref, bf16[1024,1024]{1,0:T(8,128)(2,1)} %bitcast.73, bf16[1024,1024]{1,0:T(8,128)(2,1)} %cache_ref.1, bf16[4,128,1024]{2,1,0:T(8,128)(2,1)} %shard_map.96.update_ref), custom_call_target="tpu_custom_call" | custom-call | tf_op jit(solution)/shard_map/pallas_call | solution.py:141
  (11 shorter events, 0.0 us)
Async XLA Ops:
  5.8 6.0 %copy-start.3 = (s32[4]{0:T(128)S(1)}, s32[4]{0:T(128)}, u32[]{:S(2)}) copy-start(s32[4]{0:T(128)} %param.16) | copy-start | bytes 52
  5.8 7.9 %copy-start.4 = (s32[1,2]{1,0:T(1,128)S(1)}, s32[1,2]{1,0:T(1,128)}, u32[]{:S(2)}) copy-start(s32[1,2]{1,0:T(1,128)} %param.15) | copy-start | bytes 28
  5.8 56.3 %all-to-all-start = ((bf16[128,8,1024]{2,0,1:T(8,128)(2,1)}), bf16[128,8,1024]{2,0,1:T(8,128)(2,1)S(1)}, u32[]{:S(2)}, u32[]{:S(2)}) async-start(bf16[128,8,1024]{2,0,1:T(8,128)(2,1)} %copy.20), calls=%async_computation | async-start | bytes 4194304 | tf_op jit(solution)/shard_map/all_to_all | solution.py:175
  21.8 40.3 %dynamic-slice-start = ((f32[8192]{0:T(1024)}, s32[]{:T(128)}), f32[1024]{0:T(1024)S(1)}, s32[]{:S(2)}) async-start(f32[8192]{0:T(1024)} %param.11, s32[]{:T(128)} %select_n.115), calls=%async_computation.1 | async-start | bytes 8704 | tf_op jit(solution)/shard_map/dynamic_slice | solution.py:192
  62.2 3.9 %copy-start = (bf16[128,8,1024]{2,0,1:T(8,128)(2,1)}, bf16[128,8,1024]{2,0,1:T(8,128)(2,1)S(1)}, u32[]{:S(2)}) copy-start(bf16[128,8,1024]{2,0,1:T(8,128)(2,1)S(1)} %all-to-all-done) | copy-start | bytes 6291460
  80.1 24.7 %collective-permute-start = (bf16[128,1024]{1,0:T(8,128)(2,1)S(1)}, bf16[128,1024]{1,0:T(8,128)(2,1)S(1)}, u32[]{:S(2)}, u32[]{:S(2)}) collective-permute-start(bf16[128,1024]{1,0:T(8,128)(2,1)S(1)} %fusion.16), channel_id=1, source_target_pairs={{0,0},{1,1},{2,8},{3,9},{4,16},{5,17},{6,24},{7,25},{8,2},{9,3},{1... | collective-permute-start | bytes 786440 | tf_op jit(solution)/shard_map/ppermute | solution.py:207
  104.8 0.7 copy-start.2
  141.0 9.1 %slice-start = ((s8[7340032]{0:T(1024)(128)(4,1)}), s8[4194304]{0:T(1024)(128)(4,1)S(1)}, s32[]{:S(2)}) async-start(s8[7340032]{0:T(1024)(128)(4,1)} %bitcast.89), calls=%async_computation.2 | async-start | bytes 8388608
  141.6 8.5 %slice-start.1 = ((s8[7340032]{0:T(1024)(128)(4,1)}), s8[3145728]{0:T(1024)(128)(4,1)S(1)}, s32[]{:S(2)}) async-start(s8[7340032]{0:T(1024)(128)(4,1)} %bitcast.89), calls=%async_computation.3 | async-start | bytes 6291456
  273.6 25.5 %collective-permute-start.1 = (bf16[128,1024]{1,0:T(8,128)(2,1)S(1)}, bf16[128,1024]{1,0:T(8,128)(2,1)S(1)}, u32[]{:S(2)}, u32[]{:S(2)}) collective-permute-start(bf16[128,1024]{1,0:T(8,128)(2,1)S(1)} %fusion.17), channel_id=1, source_target_pairs={{0,0},{1,1},{8,2},{9,3},{16,4},{17,5},{24,6},{25,7},{2,8},{3,9},{1... | collective-permute-start | bytes 786440 | tf_op jit(solution)/shard_map/ppermute | solution.py:227
  299.1 0.7 copy-start.1
